TPU v7x, 512 devices: a whole 4x8x8 slice. The times are simulated.
512 devices in a mesh: clip: 16 (over y_lo, z), seq: 32 (over x, y_hi, core).
Axes of the slice: x: 4, y: 8 (y_hi: 4, y_lo: 2; y = y_hi * 2 + y_lo), z: 8, core: 2. Of those that a mesh axis runs over, the one named last changes fastest.
Arguments:
- patches: bfloat16 [16, 6272, 1024], P('clip', 'seq'), may hold values from -6 to 12
- segment: int32 [16, 6272], P('clip', 'seq'), may hold values from 0 to 191, as said below
- dest_shard: int32 [16, 6144], P('clip', 'seq'), may hold values from -1 to 31, as said below
- dest_slot: int32 [16, 6144], P('clip', 'seq'), may hold values from -1 to 63, as said below
- w_qkv: bfloat16 [1024, 1536], replicated, may hold values from -1 to 4
- out_grad: bfloat16 [16, 2048, 512], P('clip', 'seq'), may hold values from -6 to 6
Outputs:
- attended: bfloat16 [16, 2048, 512], P('clip', 'seq')
- patch_grad: bfloat16 [16, 6272, 1024], P('clip', 'seq')
- weight_grad: float32 [1024, 1536], P('seq', 'clip')
Inputs may be any that keep to these rules, and one draw needn't show every extreme that they name: `segment`: within each block of 196 patches the ids start at 0, never fall and skip no value; every id names one or more patches. The number of tokens of a block is one more than its largest id. `dest_shard`: -1 exactly on the rows of a block past its number of tokens. A block of 192 rows sends at most 6 rows to each receiving block of its clip, and every receiving block gets exactly 64 rows. `dest_slot`: -1 exactly where dest_shard is -1; the rows sent to one receiving block take its rows 0 to 63 once each.
All inputs are finite; a program needn't handle non-finite values.
Results may differ from a plain program's by a relative error of at most 0.024.
Values may be sent and summed in bfloat16 or wider, within the bound.
A program may use at most 64 MiB of HBM per device.

v0:
```python
import jax
import jax.numpy as jnp
from jax import lax
from jax.sharding import PartitionSpec as P

HEADS = 8
HEAD_DIM = 64
neg_large = -1e30


def split_heads(rows_in):
    return rows_in.reshape(rows_in.shape[0], HEADS, HEAD_DIM)


def forward_fold(query_heads, running, pieces):
    scaling = HEAD_DIM ** (-0.5)
    row_max, row_total, weighted = running
    key_heads = split_heads(pieces[0])
    value_heads = split_heads(pieces[1])
    scores = (
        jnp.einsum("rhd,khd->hrk", query_heads, key_heads, preferred_element_type=jnp.float32)
        * scaling
    )
    new_max = jnp.maximum(row_max, jnp.max(scores, axis=2))
    weights = jnp.exp(scores - new_max[:, :, None])
    row_total = jnp.sum(weights, axis=2)
    weighted = jnp.einsum(
        "hrk,khd->hrd",
        weights.astype(jnp.bfloat16),
        value_heads,
        preferred_element_type=jnp.float32,
    )
    return (new_max, row_total, weighted)


def query_fold(query_heads, grad_heads, log_total, grad_dot):
    scaling = HEAD_DIM ** (-0.5)

    def combine_piece(running, pieces, offset):
        key_heads = split_heads(pieces[0])
        value_heads = split_heads(pieces[1])
        scores = (
            jnp.einsum("rhd,khd->hrk", query_heads, key_heads, preferred_element_type=jnp.float32)
            * scaling
        )
        probability = jnp.exp(scores - log_total[:, :, None])
        prob_grad = jnp.einsum(
            "rhd,khd->hrk", grad_heads, value_heads, preferred_element_type=jnp.float32
        )
        score_grad = (probability * (prob_grad - grad_dot[:, :, None])).astype(jnp.bfloat16)
        return (
            jnp.einsum("hrk,khd->hrd", score_grad, key_heads, preferred_element_type=jnp.float32)
            * scaling
        )

    return combine_piece


def key_fold(key_heads, value_heads, all_log, all_dot, pieces):
    scaling = HEAD_DIM ** (-0.5)
    piece_query = split_heads(pieces[0])
    piece_grad = split_heads(pieces[1])
    piece_log = all_log.T
    piece_dot = all_dot.T
    scores = (
        jnp.einsum("qhd,khd->hqk", piece_query, key_heads, preferred_element_type=jnp.float32)
        * scaling
    )
    probability = jnp.exp(scores - piece_log[:, :, None])
    value_grad = jnp.einsum(
        "hqk,qhd->hkd",
        probability.astype(jnp.bfloat16),
        piece_grad,
        preferred_element_type=jnp.float32,
    )
    prob_grad = jnp.einsum(
        "qhd,khd->hqk", piece_grad, value_heads, preferred_element_type=jnp.float32
    )
    score_grad = (probability * (prob_grad - piece_dot[:, :, None])).astype(jnp.bfloat16)
    key_grad = (
        jnp.einsum("hqk,qhd->hkd", score_grad, piece_query, preferred_element_type=jnp.float32)
        * scaling
    )
    return (key_grad, value_grad)


def head_rows(matrix):
    return matrix.transpose(1, 0, 2).reshape(matrix.shape[1], HEADS * HEAD_DIM)


def local(patches, segment, dest_shard, dest_slot, w_qkv, out_grad):
    shard_count = lax.axis_size("seq")
    patch_rows = patches[0]
    patch_token = segment[0]
    targets = dest_shard[0]
    slot_ids = dest_slot[0]
    token_cap = targets.shape[0]
    pair_cap = token_cap // shard_count
    local_rows = out_grad.shape[1]
    inner_width = HEADS * HEAD_DIM
    member = (
        lax.broadcasted_iota(jnp.int32, (token_cap, patch_token.shape[0]), 0)
        == patch_token[None, :]
    )
    member_half = member.astype(jnp.bfloat16)
    counts = jnp.sum(member.astype(jnp.float32), axis=1)
    token_sums = jnp.dot(member_half, patch_rows, preferred_element_type=jnp.float32)
    tokens = (token_sums / jnp.maximum(counts, 1.0)[:, None]).astype(jnp.bfloat16)
    to_shard = (
        targets[:, None] == lax.broadcasted_iota(jnp.int32, (token_cap, shard_count), 1)
    ).astype(jnp.int32)
    ranking = jnp.sum((jnp.cumsum(to_shard, axis=0) - 1) * to_shard, axis=1)
    position = jnp.where(targets >= 0, targets * pair_cap + ranking, -1)
    chooser = position[None, :] == lax.broadcasted_iota(
        jnp.int32, (shard_count * pair_cap, token_cap), 0
    )
    chooser_half = chooser.astype(jnp.bfloat16)
    send_rows = jnp.dot(chooser_half, tokens, preferred_element_type=jnp.float32).astype(
        jnp.bfloat16
    )
    send_slot = jnp.sum(chooser.astype(jnp.int32) * (slot_ids + 1)[None, :], axis=1) - 1
    came_rows, came_slot = (
        lax.all_to_all(
            send_rows.reshape(shard_count, pair_cap, -1),
            "seq",
            split_axis=0,
            concat_axis=0,
            tiled=True,
        ),
        lax.all_to_all(
            send_slot.reshape(shard_count, pair_cap), "seq", split_axis=0, concat_axis=0, tiled=True
        ),
    )
    came_slot = came_slot.reshape(-1)
    placer = (
        came_slot[None, :]
        == lax.broadcasted_iota(jnp.int32, (local_rows, shard_count * pair_cap), 0)
    ).astype(jnp.bfloat16)
    placed = jnp.dot(
        placer, came_rows.reshape(shard_count * pair_cap, -1), preferred_element_type=jnp.float32
    ).astype(jnp.bfloat16)
    projected = jnp.dot(placed, w_qkv, preferred_element_type=jnp.float32).astype(jnp.bfloat16)
    query_rows = projected[:, :inner_width]
    key_rows = projected[:, inner_width : 2 * inner_width]
    value_rows = projected[:, 2 * inner_width :]
    query_heads = split_heads(query_rows)
    initial = (
        jnp.full((HEADS, local_rows), neg_large, jnp.float32),
        jnp.zeros((HEADS, local_rows), jnp.float32),
        jnp.zeros((HEADS, local_rows, HEAD_DIM), jnp.float32),
    )
    row_max, row_total, weighted = forward_fold(
        query_heads,
        initial,
        (
            lax.all_gather(key_rows, "seq", axis=0, tiled=True),
            lax.all_gather(value_rows, "seq", axis=0, tiled=True),
        ),
    )
    attended_rows = head_rows((weighted / row_total[:, :, None]).astype(jnp.bfloat16))
    grad_rows = out_grad[0]
    grad_heads = split_heads(grad_rows)
    log_total = row_max + jnp.log(row_total)
    grad_dot = jnp.sum(
        grad_heads.astype(jnp.float32) * split_heads(attended_rows).astype(jnp.float32), axis=2
    )
    blank = jnp.zeros((HEADS, local_rows, HEAD_DIM), jnp.float32)
    query_step = query_fold(query_heads, grad_heads, log_total, grad_dot.T)
    query_grad = query_step(
        blank,
        (
            lax.all_gather(key_rows, "seq", axis=0, tiled=True),
            lax.all_gather(value_rows, "seq", axis=0, tiled=True),
        ),
        jnp.int32(0),
    )
    all_log, all_dot = (
        lax.all_gather(log_total.T, "seq", axis=0, tiled=True),
        lax.all_gather(grad_dot, "seq", axis=0, tiled=True),
    )
    key_grad, value_grad = key_fold(
        split_heads(key_rows),
        split_heads(value_rows),
        all_log,
        all_dot,
        (
            lax.all_gather(query_rows, "seq", axis=0, tiled=True),
            lax.all_gather(grad_rows, "seq", axis=0, tiled=True),
        ),
    )
    proj_grad = jnp.concatenate(
        [head_rows(query_grad), head_rows(key_grad), head_rows(value_grad)], axis=1
    ).astype(jnp.bfloat16)
    placed_grad = jnp.einsum(
        "rc,dc->rd", proj_grad, w_qkv, preferred_element_type=jnp.float32
    ).astype(jnp.bfloat16)
    partial_value = jnp.einsum(
        "rd,rc->dc", placed, proj_grad, preferred_element_type=jnp.float32
    ).astype(jnp.bfloat16)
    across = lax.psum_scatter(partial_value, "seq", scatter_dimension=0, tiled=True).astype(
        jnp.float32
    )
    weight_grad = lax.psum_scatter(
        across.astype(jnp.bfloat16), "clip", scatter_dimension=1, tiled=True
    ).astype(jnp.float32)
    back_rows = jnp.einsum(
        "rj,rd->jd", placer, placed_grad, preferred_element_type=jnp.float32
    ).astype(jnp.bfloat16)
    returned = lax.all_to_all(
        back_rows.reshape(shard_count, pair_cap, -1), "seq", split_axis=0, concat_axis=0, tiled=True
    )
    token_grad = jnp.einsum(
        "jt,jd->td",
        chooser_half,
        returned.reshape(shard_count * pair_cap, -1),
        preferred_element_type=jnp.float32,
    ).astype(jnp.bfloat16)
    patch_sums = jnp.einsum(
        "tp,td->pd", member_half, token_grad, preferred_element_type=jnp.float32
    )
    patch_count = jnp.sum(member.astype(jnp.float32) * counts[:, None], axis=0)
    patch_grad = (patch_sums / patch_count[:, None]).astype(jnp.bfloat16)
    return (attended_rows[None], patch_grad[None], weight_grad)


def solution(mesh):
    return jax.shard_map(
        local,
        mesh=mesh,
        in_specs=(
            P("clip", "seq", None),
            P("clip", "seq"),
            P("clip", "seq"),
            P("clip", "seq"),
            P(),
            P("clip", "seq", None),
        ),
        out_specs=(P("clip", "seq", None), P("clip", "seq", None), P("seq", "clip")),
        check_vma=False,
    )
```

profile of v0, /device:TPU:2, one launch (start us, length us, event | category | flops | bytes accessed | tf_op | source)
XLA Modules:
  0.0 507.5 jit_solution(14821409125250477801)
XLA Ops:
  13.2 10.3 %all-to-all-start = ((s32[32,1,6]{2,1,0:T(1,128)}), s32[32,1,6]{2,1,0:T(1,128)S(1)}, u32[]{:S(2)}, u32[]{:S(2)}) async-start(s32[32,1,6]{2,1,0:T(1,128)} %bitcast.5), calls=%async_computation | async-start | bytes 32768 | tf_op jit(solution)/shard_map/all_to_all | solution.py:130
  27.9 4.2 all-to-all-done
  32.0 5.7 %all-to-all-start.1 = ((bf16[32,6,1024]{2,1,0:T(8,128)(2,1)}), bf16[32,6,1024]{2,1,0:T(8,128)(2,1)}, u32[]{:S(2)}, u32[]{:S(2)}) async-start(bf16[32,6,1024]{2,1,0:T(8,128)(2,1)} %reshape.104), calls=%async_computation.1 | async-start | bytes 1048576 | tf_op jit(solution)/shard_map/all_to_all | solution.py:123
  39.1 15.6 %all-to-all-done.1 = bf16[32,6,1024]{2,1,0:T(8,128)(2,1)} async-done(((bf16[32,6,1024]{2,1,0:T(8,128)(2,1)}), bf16[32,6,1024]{2,1,0:T(8,128)(2,1)}, u32[]{:S(2)}, u32[]{:S(2)}) %all-to-all-start.1) | async-done | bytes 393248 | tf_op jit(solution)/shard_map/all_to_all | solution.py:123
  62.2 1.6 reshape.112
  63.8 13.4 %all-gather.14.cloned.1.call-done = bf16[1,2048,512]{2,1,0:T(8,128)(2,1)} async-done(((bf16[1,64,512]{2,1,0:T(8,128)(2,1)}), bf16[1,2048,512]{2,1,0:T(8,128)(2,1)}) %all-gather.14.cloned.1.call-update) | async-done | bytes 2097168 | tf_op jit(solution)/shard_map/all_gather | solution.py:188
  77.3 3.9 copy.62
  81.2 56.0 %all-gather.8.cloned.1.call-done = bf16[2048,512]{1,0:T(8,128)(2,1)} async-done(((bf16[64,512]{1,0:T(8,128)(2,1)}), bf16[2048,512]{1,0:T(8,128)(2,1)}) %all-gather.8.cloned.1.call-update) | async-done | bytes 2097168 | tf_op jit(solution)/shard_map/all_gather | solution.py:156
  137.3 3.9 copy.53
  141.2 56.1 %all-gather.10.cloned.1.call-done = bf16[2048,512]{1,0:T(8,128)(2,1)} async-done(((bf16[64,512]{1,0:T(8,128)(2,1)}), bf16[2048,512]{1,0:T(8,128)(2,1)}) %all-gather.10.cloned.1.call-update) | async-done | bytes 2097168 | tf_op jit(solution)/shard_map/all_gather | solution.py:157
  197.3 4.0 copy.55
  201.2 2.4 multiply_reduce_fusion
  205.1 1.6 copy-done.4
  206.7 1.6 multiply_reduce_fusion.1
  208.3 5.2 %fusion.28 = bf16[64,8,64]{2,0,1:T(8,128)(2,1)S(1)} fusion(bf16[2048,8,64]{0,2,1:T(8,128)(2,1)} %bitcast.106, f32[8,64,2048]{2,1,0:T(8,128)} %copy-done.1, bf16[2048,8,64]{0,2,1:T(8,128)(2,1)} %bitcast.107, bf16[64,8,64]{0,2,1:T(8,128)(2,1)S(1)} %bitcast.114, f32[8,64]{1,0:T(8,128)S(1)} %bitcast.120, f32[8,64]{1,0:T(8,128)} %log_add_fusion), kind=kOutput, calls=%fused_computation.36 | convolution fusion | flops 273743872 | bytes 8523776 | tf_op jit(solution)/shard_map/hrk,khd->hrd/dot_general | solution.py:52
  214.5 38.9 %all-gather.2 = f32[32,64,8]{1,2,0:T(8,128)S(1)} all-gather(f32[1,64,8]{1,2,0:T(8,128)S(1)} %bitcast.121), channel_id=1, replica_groups=mesh['clip'=16,'seq'=32] {'seq'}, dimensions={0}, use_global_device_ids=true | all-gather | bytes 67584 | tf_op jit(solution)/shard_map/all_gather | solution.py:179
  254.2 40.2 %all-gather.1 = f32[32,64,8]{1,2,0:T(8,128)S(1)} all-gather(f32[1,64,8]{1,2,0:T(8,128)S(1)} %fusion.58), channel_id=1, replica_groups=mesh['clip'=16,'seq'=32] {'seq'}, dimensions={0}, use_global_device_ids=true | all-gather | bytes 67584 | tf_op jit(solution)/shard_map/all_gather | solution.py:178
  295.4 4.0 copy.59
  299.3 2.4 fusion.44
  301.8 2.0 fusion.30
  303.8 5.9 %fusion.29 = bf16[64,8,64]{2,0,1:T(8,128)(2,1)} fusion(bf16[2048,8,64]{0,2,1:T(8,128)(2,1)} %bitcast.104, f32[8,2048,64]{1,2,0:T(8,128)} %copy-done.2, bf16[2048,8,64]{0,2,1:T(8,128)(2,1)} %bitcast.101, f32[8,2048]{1,0:T(8,128)} %bitcast.115, f32[8,2048]{1,0:T(8,128)S(1)} %bitcast.111, bf16[64,8,64]{2,1,0:T(8,128)(2,1)} %reshape.112), kind=kOutput, calls=%fused_computation.37 | convolution fusion | flops 273743872 | bytes 8650752 | tf_op jit(solution)/shard_map/hqk,qhd->hkd/dot_general | solution.py:81
  309.6 1.6 copy.65
  312.3 1.6 copy.66
  314.0 1.7 reshape.115
  316.5 2.6 convolution_convert_fusion
  319.2 2.2 convolution_convert_fusion.3
  322.3 10.2 %all-to-all-start.2 = ((bf16[32,6,1024]{2,1,0:T(8,128)(2,1)}), bf16[32,6,1024]{2,1,0:T(8,128)(2,1)}, u32[]{:S(2)}, u32[]{:S(2)}) async-start(bf16[32,6,1024]{2,1,0:T(8,128)(2,1)} %reshape.116), calls=%async_computation.2 | async-start | bytes 1048576 | tf_op jit(solution)/shard_map/all_to_all | solution.py:209
  332.7 1.6 copy.67
  334.4 13.7 %all-to-all-done.2 = bf16[32,6,1024]{2,1,0:T(8,128)(2,1)} async-done(((bf16[32,6,1024]{2,1,0:T(8,128)(2,1)}), bf16[32,6,1024]{2,1,0:T(8,128)(2,1)}, u32[]{:S(2)}, u32[]{:S(2)}) %all-to-all-start.2) | async-done | bytes 393248 | tf_op jit(solution)/shard_map/all_to_all | solution.py:209
  349.2 74.2 %reduce-scatter.5.cloned.1.call-done = bf16[32,1536]{1,0:T(8,128)(2,1)} async-done(((bf16[1024,1536]{1,0:T(8,128)(2,1)}), bf16[32,1536]{1,0:T(8,128)(2,1)}) %reduce-scatter.5.cloned.1.call-update) | async-done | bytes 98320 | tf_op jit(solution)/shard_map/reduce_scatter | solution.py:200
  423.4 1.8 copy.69
  426.5 72.7 %reduce-scatter.7.cloned.1.call-done = bf16[96,32]{1,0:T(8,128)(2,1)} async-done(((bf16[1536,32]{1,0:T(8,128)(2,1)}), bf16[96,32]{1,0:T(8,128)(2,1)}) %reduce-scatter.7.cloned.1.call-update) | async-done | bytes 6160
  (89 shorter events, 30.1 us)
Async XLA Ops:
  7.2 49.6 %copy-start = (bf16[1024,1536]{1,0:T(8,128)(2,1)S(1)}, bf16[1024,1536]{1,0:T(8,128)(2,1)}, u32[]{:S(2)}) copy-start(bf16[1024,1536]{1,0:T(8,128)(2,1)} %param.10) | copy-start | bytes 9437188
  7.2 70.1 %all-gather.14.cloned.1.call-start = ((), (), s32[]{:S(2)}) async-start(), calls=%async_computation.9 | async-start | bytes 2162688 | tf_op jit(solution)/shard_map/all_gather | solution.py:188
  11.8 0.6 copy-start.12
  13.2 18.8 %all-to-all-start = ((s32[32,1,6]{2,1,0:T(1,128)}), s32[32,1,6]{2,1,0:T(1,128)S(1)}, u32[]{:S(2)}, u32[]{:S(2)}) async-start(s32[32,1,6]{2,1,0:T(1,128)} %bitcast.5), calls=%async_computation | async-start | bytes 32768 | tf_op jit(solution)/shard_map/all_to_all | solution.py:130
  24.3 0.6 copy-start.10
  32.0 22.7 %all-to-all-start.1 = ((bf16[32,6,1024]{2,1,0:T(8,128)(2,1)}), bf16[32,6,1024]{2,1,0:T(8,128)(2,1)}, u32[]{:S(2)}, u32[]{:S(2)}) async-start(bf16[32,6,1024]{2,1,0:T(8,128)(2,1)} %reshape.104), calls=%async_computation.1 | async-start | bytes 1048576 | tf_op jit(solution)/shard_map/all_to_all | solution.py:123
  37.7 99.5 %all-gather.8.cloned.1.call-start = ((), (), s32[]{:S(2)}) async-start(), calls=%async_computation.5 | async-start | bytes 2162688 | tf_op jit(solution)/shard_map/all_gather | solution.py:156
  56.1 0.7 copy-start.5
  56.8 2.7 copy-start.8
  58.1 139.2 %all-gather.10.cloned.1.call-start = ((), (), s32[]{:S(2)}) async-start(), calls=%async_computation.6 | async-start | bytes 2162688 | tf_op jit(solution)/shard_map/all_gather | solution.py:157
  58.8 236.5 %all-gather.12.cloned.1.call-start = ((), (), s32[]{:S(2)}) async-start(), calls=%async_computation.7 | async-start | bytes 2162688 | tf_op jit(solution)/shard_map/all_gather | solution.py:187
  59.4 364.0 %reduce-scatter.5.cloned.1.call-start = ((), (), s32[]{:S(2)}) async-start(), calls=%async_computation.8 | async-start | bytes 3244032 | tf_op jit(solution)/shard_map/reduce_scatter | solution.py:200
  203.6 4.8 copy-start.1
  203.6 3.1 copy-start.4
  203.6 3.1 copy-start.9
  299.3 2.4 copy-start.3
  301.8 2.0 copy-start.2
  303.8 12.7 %copy-start.6 = (bf16[64,1024]{1,0:T(8,128)(2,1)S(1)}, bf16[64,1024]{1,0:T(8,128)(2,1)}, u32[]{:S(2)}) copy-start(bf16[64,1024]{1,0:T(8,128)(2,1)} %copy-done.5) | copy-start | bytes 393220
  316.5 2.7 copy-start.7
  319.2 13.4 %copy-start.11 = (f32[192]{0:T(256)S(1)}, f32[192]{0:T(256)}, u32[]{:S(2)}) copy-start(f32[192]{0:T(256)} %copy-done.10) | copy-start | bytes 2308
  319.2 13.4 %copy-start.14 = (s32[1,196]{1,0:T(1,128)S(1)}, s32[1,196]{1,0:T(1,128)}, u32[]{:S(2)}) copy-start(s32[1,196]{1,0:T(1,128)} %param.7) | copy-start | bytes 2356
  319.2 106.0 %copy-start.13 = (s32[1,192]{1,0:T(1,128)S(1)}, s32[1,192]{1,0:T(1,128)}, u32[]{:S(2)}) copy-start(s32[1,192]{1,0:T(1,128)} %copy-done.12) | copy-start | bytes 2308
  322.3 25.7 %all-to-all-start.2 = ((bf16[32,6,1024]{2,1,0:T(8,128)(2,1)}), bf16[32,6,1024]{2,1,0:T(8,128)(2,1)}, u32[]{:S(2)}, u32[]{:S(2)}) async-start(bf16[32,6,1024]{2,1,0:T(8,128)(2,1)} %reshape.116), calls=%async_computation.2 | async-start | bytes 1048576 | tf_op jit(solution)/shard_map/all_to_all | solution.py:209
  332.6 166.7 %reduce-scatter.7.cloned.1.call-start = ((), (), s32[]{:S(2)}) async-start(), calls=%async_computation.10 | async-start | bytes 417792
Sparse Core Ops, SparseCore 0:
  11.1 66.1 all-gather.13
  80.4 56.8 all-gather.7
  140.4 56.8 all-gather.9
  200.8 56.8 all-gather.11
  319.3 104.0 reduce-scatter.4
  426.1 73.1 reduce-scatter.6
where the time goes:
time: 509 us; the launch traced here: 508 us
  waiting for transfers between devices  308 us (61%)
  blocking collectives  79.2 us (16%)
  local copies, waits for them, and re-layouts  43.7 us (9%)
  matrix products  27.9 us (5%)
  starting transfers between devices  26.4 us (5%)
  between operations  14.4 us (3%)
  other arithmetic  8.04 us (2%)
    unnamed x7, waiting for transfers between devices  74.7 us
    reduce_scatter x1, waiting for transfers between devices, local(): lax.psum_scatter(partial_value, 'seq', scatter_dimension=0, tiled=True)  74.2 us
    all_gather x1, waiting for transfers between devices, local(): lax.all_gather(value_rows, 'seq', axis=0, tiled=True)  56.1 us
    all_gather x1, waiting for transfers between devices, local(): lax.all_gather(key_rows, 'seq', axis=0, tiled=True)  56 us
    all_gather x1, blocking collectives, local(): lax.all_gather(log_total.T, 'seq', axis=0, tiled=True)  40.2 us
    all_gather x1, blocking collectives, local(): lax.all_gather(grad_dot, 'seq', axis=0, tiled=True)  38.9 us
    all_to_all x1, waiting for transfers between devices, local(): lax.all_to_all(send_rows.reshape(shard_count, pair_cap, -1), 'seq', split...  15.6 us
    all_to_all x1, waiting for transfers between devices, local(): lax.all_to_all(back_rows.reshape(shard_count, pair_cap, -1), 'seq', split...  13.7 us
  transfers between devices with their start and end apart: 9, of which 8 were waited for; matrix products, arithmetic and copies ran while one was open for 10% of the time, Pallas kernels for 0%

commit v1 on v0

--- a/solution.py
+++ b/solution.py
@@ -176,7 +176,9 @@
     )
     all_log, all_dot = (
         lax.all_gather(log_total.T, "seq", axis=0, tiled=True),
-        lax.all_gather(grad_dot, "seq", axis=0, tiled=True),
+        jnp.concatenate(
+            lax.all_to_all(jnp.stack([grad_dot] * lax.axis_size("seq")), "seq", 0, 0), axis=0
+        ),
     )
     key_grad, value_grad = key_fold(
         split_heads(key_rows),

time: 509 us -> 481 us (0.945)
  blocking collectives: 79.2 us -> 40.2 us
  starting transfers between devices: 26.4 us -> 33.4 us
    all_gather x1 -> x0, blocking collectives: 38.9 us -> none  [local(): lax.all_gather(grad_dot, 'seq', axis=0, tiled=True)]
    all_to_all x0 -> x1, starting transfers between devices: none -> 7.18 us  [local(): lax.all_to_all(jnp.stack([grad_dot] * lax.axis_size('seq')), 'seq', 0, 0)]
    unnamed x38 -> x42, local copies, waits for them, and re-layouts: 10.2 us -> 12.7 us
  transfers between devices with their start and end apart: 9 -> 10, of which waited for: 8 -> 8; matrix products, arithmetic and copies ran while one was open for 10% -> 12% of each run, Pallas kernels for 0% -> 0%
where the time goes in v1:
time: 481 us; the launch traced here: 479 us
  waiting for transfers between devices  307 us (64%)
  local copies, waits for them, and re-layouts  46.6 us (10%)
  blocking collectives  40.2 us (8%)
  starting transfers between devices  33.4 us (7%)
  matrix products  27.5 us (6%)
  between operations  14.4 us (3%)
  other arithmetic  9.69 us (2%)
    unnamed x7, waiting for transfers between devices  74.9 us
    reduce_scatter x1, waiting for transfers between devices, local(): lax.psum_scatter(partial_value, 'seq', scatter_dimension=0, tiled=True)  73 us
    all_gather x1, waiting for transfers between devices, local(): lax.all_gather(key_rows, 'seq', axis=0, tiled=True)  56.3 us
    all_gather x1, waiting for transfers between devices, local(): lax.all_gather(value_rows, 'seq', axis=0, tiled=True)  56 us
    all_gather x1, blocking collectives, local(): lax.all_gather(log_total.T, 'seq', axis=0, tiled=True)  40.2 us
    all_to_all x1, waiting for transfers between devices, local(): lax.all_to_all(send_rows.reshape(shard_count, pair_cap, -1), 'seq', split...  15.7 us
    all_to_all x1, waiting for transfers between devices, local(): lax.all_to_all(back_rows.reshape(shard_count, pair_cap, -1), 'seq', split...  13.9 us
    all_gather x1, waiting for transfers between devices, local(): lax.all_gather(grad_rows, 'seq', axis=0, tiled=True)  13.5 us
  transfers between devices with their start and end apart: 10, of which 8 were waited for; matrix products, arithmetic and copies ran while one was open for 12% of the time, Pallas kernels for 0%

profile of v1, /device:TPU:2, one launch (start us, length us, event | category | flops | bytes accessed | tf_op | source)
XLA Modules:
  0.0 479.3 jit_solution(8494886509361190464)
XLA Ops:
  13.2 10.3 %all-to-all-start = ((s32[32,1,6]{2,1,0:T(1,128)}), s32[32,1,6]{2,1,0:T(1,128)S(1)}, u32[]{:S(2)}, u32[]{:S(2)}) async-start(s32[32,1,6]{2,1,0:T(1,128)} %bitcast.5), calls=%async_computation | async-start | bytes 32768 | tf_op jit(solution)/shard_map/all_to_all | solution.py:130
  25.3 1.5 convolution_convert_fusion.4
  27.8 4.2 all-to-all-done
  32.0 5.7 %all-to-all-start.1 = ((bf16[32,6,1024]{2,1,0:T(8,128)(2,1)}), bf16[32,6,1024]{2,1,0:T(8,128)(2,1)}, u32[]{:S(2)}, u32[]{:S(2)}) async-start(bf16[32,6,1024]{2,1,0:T(8,128)(2,1)} %reshape.109), calls=%async_computation.1 | async-start | bytes 1048576 | tf_op jit(solution)/shard_map/all_to_all | solution.py:123
  39.0 15.7 %all-to-all-done.1 = bf16[32,6,1024]{2,1,0:T(8,128)(2,1)} async-done(((bf16[32,6,1024]{2,1,0:T(8,128)(2,1)}), bf16[32,6,1024]{2,1,0:T(8,128)(2,1)}, u32[]{:S(2)}, u32[]{:S(2)}) %all-to-all-start.1) | async-done | bytes 393248 | tf_op jit(solution)/shard_map/all_to_all | solution.py:123
  62.1 1.6 reshape.117
  63.7 13.5 %all-gather.13.cloned.1.call-done = bf16[1,2048,512]{2,1,0:T(8,128)(2,1)} async-done(((bf16[1,64,512]{2,1,0:T(8,128)(2,1)}), bf16[1,2048,512]{2,1,0:T(8,128)(2,1)}) %all-gather.13.cloned.1.call-update) | async-done | bytes 2097168 | tf_op jit(solution)/shard_map/all_gather | solution.py:190
  77.2 3.9 copy.79
  81.2 56.3 %all-gather.7.cloned.1.call-done = bf16[2048,512]{1,0:T(8,128)(2,1)} async-done(((bf16[64,512]{1,0:T(8,128)(2,1)}), bf16[2048,512]{1,0:T(8,128)(2,1)}) %all-gather.7.cloned.1.call-update) | async-done | bytes 2097168 | tf_op jit(solution)/shard_map/all_gather | solution.py:156
  137.5 4.0 copy.70
  141.4 56.0 %all-gather.9.cloned.1.call-done = bf16[2048,512]{1,0:T(8,128)(2,1)} async-done(((bf16[64,512]{1,0:T(8,128)(2,1)}), bf16[2048,512]{1,0:T(8,128)(2,1)}) %all-gather.9.cloned.1.call-update) | async-done | bytes 2097168 | tf_op jit(solution)/shard_map/all_gather | solution.py:157
  197.5 3.9 copy.72
  201.4 2.4 multiply_reduce_fusion
  204.6 2.2 copy-done.4
  206.9 1.6 multiply_reduce_fusion.1
  209.3 7.2 %all-to-all-start.2 = ((f32[32,1,512]{2,1,0:T(1,128)}), f32[32,1,512]{2,1,0:T(1,128)}, u32[]{:S(2)}, u32[]{:S(2)}) async-start(f32[32,1,512]{2,1,0:T(1,128)} %reshape.141), calls=%async_computation.2 | async-start | bytes 131072 | tf_op jit(solution)/shard_map/all_to_all | solution.py:180
  216.5 40.2 %all-gather.1 = f32[32,64,8]{1,2,0:T(8,128)S(1)} all-gather(f32[1,64,8]{1,2,0:T(8,128)S(1)} %fusion.58), channel_id=1, replica_groups=mesh['clip'=16,'seq'=32] {'seq'}, dimensions={0}, use_global_device_ids=true | all-gather | bytes 67584 | tf_op jit(solution)/shard_map/all_gather | solution.py:178
  256.8 5.9 %fusion.28 = bf16[64,8,64]{2,0,1:T(8,128)(2,1)} fusion(bf16[2048,8,64]{0,2,1:T(8,128)(2,1)} %bitcast.108, f32[8,64,2048]{2,1,0:T(8,128)} %copy-done.2, bf16[2048,8,64]{0,2,1:T(8,128)(2,1)} %bitcast.109, bf16[64,8,64]{0,2,1:T(8,128)(2,1)} %bitcast.116, f32[8,64]{1,0:T(8,128)S(1)} %bitcast.123, f32[8,64]{1,0:T(8,128)S(1)} %log_add_fusion), kind=kOutput, calls=%fused_computation.36 | convolution fusion | flops 273743872 | bytes 8523776 | tf_op jit(solution)/shard_map/hrk,khd->hrd/dot_general | solution.py:52
  262.8 4.0 copy.76
  266.8 2.4 fusion.44
  274.2 2.3 reduce.6
  278.1 1.6 reshape.119
  279.7 5.9 %fusion.29 = bf16[64,8,64]{2,0,1:T(8,128)(2,1)} fusion(bf16[2048,8,64]{0,2,1:T(8,128)(2,1)} %bitcast.106, f32[8,2048,64]{1,2,0:T(8,128)} %copy-done.1, bf16[2048,8,64]{0,2,1:T(8,128)(2,1)} %bitcast.103, f32[8,2048]{1,0:T(8,128)} %bitcast.118, f32[8,2048]{1,0:T(8,128)S(1)} %bitcast.114, bf16[64,8,64]{2,1,0:T(8,128)(2,1)} %reshape.117), kind=kOutput, calls=%fused_computation.37 | convolution fusion | flops 273743872 | bytes 8650752 | tf_op jit(solution)/shard_map/hqk,qhd->hkd/dot_general | solution.py:81
  285.6 1.6 copy.82
  289.1 2.6 convolution_convert_fusion
  291.8 2.2 convolution_convert_fusion.3
  295.0 10.1 %all-to-all-start.3 = ((bf16[32,6,1024]{2,1,0:T(8,128)(2,1)}), bf16[32,6,1024]{2,1,0:T(8,128)(2,1)}, u32[]{:S(2)}, u32[]{:S(2)}) async-start(bf16[32,6,1024]{2,1,0:T(8,128)(2,1)} %reshape.122), calls=%async_computation.3 | async-start | bytes 1048576 | tf_op jit(solution)/shard_map/all_to_all | solution.py:211
  305.2 1.6 copy.84
  306.8 13.9 %all-to-all-done.3 = bf16[32,6,1024]{2,1,0:T(8,128)(2,1)} async-done(((bf16[32,6,1024]{2,1,0:T(8,128)(2,1)}), bf16[32,6,1024]{2,1,0:T(8,128)(2,1)}, u32[]{:S(2)}, u32[]{:S(2)}) %all-to-all-start.3) | async-done | bytes 393248 | tf_op jit(solution)/shard_map/all_to_all | solution.py:211
  321.9 73.0 %reduce-scatter.5.cloned.1.call-done = bf16[32,1536]{1,0:T(8,128)(2,1)} async-done(((bf16[1024,1536]{1,0:T(8,128)(2,1)}), bf16[32,1536]{1,0:T(8,128)(2,1)}) %reduce-scatter.5.cloned.1.call-update) | async-done | bytes 98320 | tf_op jit(solution)/shard_map/reduce_scatter | solution.py:202
  394.9 1.8 copy.86
  398.0 72.9 %reduce-scatter.7.cloned.1.call-done = bf16[96,32]{1,0:T(8,128)(2,1)} async-done(((bf16[1536,32]{1,0:T(8,128)(2,1)}), bf16[96,32]{1,0:T(8,128)(2,1)}) %reduce-scatter.7.cloned.1.call-update) | async-done | bytes 6160
  (97 shorter events, 32.8 us)
Async XLA Ops:
  7.2 49.5 %copy-start = (bf16[1024,1536]{1,0:T(8,128)(2,1)S(1)}, bf16[1024,1536]{1,0:T(8,128)(2,1)}, u32[]{:S(2)}) copy-start(bf16[1024,1536]{1,0:T(8,128)(2,1)} %param.10) | copy-start | bytes 9437188
  7.2 70.1 %all-gather.13.cloned.1.call-start = ((), (), s32[]{:S(2)}) async-start(), calls=%async_computation.10 | async-start | bytes 2162688 | tf_op jit(solution)/shard_map/all_gather | solution.py:190
  11.8 0.5 copy-start.13
  13.2 18.8 %all-to-all-start = ((s32[32,1,6]{2,1,0:T(1,128)}), s32[32,1,6]{2,1,0:T(1,128)S(1)}, u32[]{:S(2)}, u32[]{:S(2)}) async-start(s32[32,1,6]{2,1,0:T(1,128)} %bitcast.5), calls=%async_computation | async-start | bytes 32768 | tf_op jit(solution)/shard_map/all_to_all | solution.py:130
  24.2 0.5 copy-start.11
  32.0 22.7 %all-to-all-start.1 = ((bf16[32,6,1024]{2,1,0:T(8,128)(2,1)}), bf16[32,6,1024]{2,1,0:T(8,128)(2,1)}, u32[]{:S(2)}, u32[]{:S(2)}) async-start(bf16[32,6,1024]{2,1,0:T(8,128)(2,1)} %reshape.109), calls=%async_computation.1 | async-start | bytes 1048576 | tf_op jit(solution)/shard_map/all_to_all | solution.py:123
  37.6 99.8 %all-gather.7.cloned.1.call-start = ((), (), s32[]{:S(2)}) async-start(), calls=%async_computation.6 | async-start | bytes 2162688 | tf_op jit(solution)/shard_map/all_gather | solution.py:156
  56.0 0.7 copy-start.5
  56.7 2.7 copy-start.8
  58.1 139.4 %all-gather.9.cloned.1.call-start = ((), (), s32[]{:S(2)}) async-start(), calls=%async_computation.7 | async-start | bytes 2162688 | tf_op jit(solution)/shard_map/all_gather | solution.py:157
  58.8 204.0 %all-gather.11.cloned.1.call-start = ((), (), s32[]{:S(2)}) async-start(), calls=%async_computation.8 | async-start | bytes 2162688 | tf_op jit(solution)/shard_map/all_gather | solution.py:189
  203.8 4.8 copy-start.2
  203.8 3.1 copy-start.4
  203.8 3.1 copy-start.9
  209.3 64.4 %all-to-all-start.2 = ((f32[32,1,512]{2,1,0:T(1,128)}), f32[32,1,512]{2,1,0:T(1,128)}, u32[]{:S(2)}, u32[]{:S(2)}) async-start(f32[32,1,512]{2,1,0:T(1,128)} %reshape.141), calls=%async_computation.2 | async-start | bytes 131072 | tf_op jit(solution)/shard_map/all_to_all | solution.py:180
  216.5 178.4 %reduce-scatter.5.cloned.1.call-start = ((), (), s32[]{:S(2)}) async-start(), calls=%async_computation.9 | async-start | bytes 3244032 | tf_op jit(solution)/shard_map/reduce_scatter | solution.py:202
  266.8 2.4 copy-start.3
  269.2 1.9 copy-start.1
  269.2 1.9 copy-start.10
  279.7 9.4 %copy-start.6 = (bf16[64,1024]{1,0:T(8,128)(2,1)S(1)}, bf16[64,1024]{1,0:T(8,128)(2,1)}, u32[]{:S(2)}) copy-start(bf16[64,1024]{1,0:T(8,128)(2,1)} %copy-done.5) | copy-start | bytes 393220
  289.1 2.7 copy-start.7
  291.8 13.3 %copy-start.12 = (f32[192]{0:T(256)S(1)}, f32[192]{0:T(256)}, u32[]{:S(2)}) copy-start(f32[192]{0:T(256)} %copy-done.11) | copy-start | bytes 2308
  291.8 13.3 %copy-start.15 = (s32[1,196]{1,0:T(1,128)S(1)}, s32[1,196]{1,0:T(1,128)}, u32[]{:S(2)}) copy-start(s32[1,196]{1,0:T(1,128)} %param.7) | copy-start | bytes 2356
  291.8 104.9 %copy-start.14 = (s32[1,192]{1,0:T(1,128)S(1)}, s32[1,192]{1,0:T(1,128)}, u32[]{:S(2)}) copy-start(s32[1,192]{1,0:T(1,128)} %copy-done.13) | copy-start | bytes 2308
  295.0 25.8 %all-to-all-start.3 = ((bf16[32,6,1024]{2,1,0:T(8,128)(2,1)}), bf16[32,6,1024]{2,1,0:T(8,128)(2,1)}, u32[]{:S(2)}, u32[]{:S(2)}) async-start(bf16[32,6,1024]{2,1,0:T(8,128)(2,1)} %reshape.122), calls=%async_computation.3 | async-start | bytes 1048576 | tf_op jit(solution)/shard_map/all_to_all | solution.py:211
  305.0 165.9 %reduce-scatter.7.cloned.1.call-start = ((), (), s32[]{:S(2)}) async-start(), calls=%async_computation.11 | async-start | bytes 417792
Sparse Core Ops, SparseCore 0:
  11.1 66.0 all-gather.12
  80.4 57.0 all-gather.6
  140.6 56.8 all-gather.8
  201.0 57.0 all-gather.10
  291.9 102.9 reduce-scatter.4
  397.6 73.3 reduce-scatter.6
